TPU v7x, 32 devices: a whole 2x2x4 slice. The times are simulated.
32 devices in a mesh: dp: 2 (over x), row: 4 (over y, core), col: 4 (over z).
Axes of the slice: x: 2, y: 2, z: 4, core: 2. Of those that a mesh axis runs over, the one named last changes fastest.
Arguments:
- tokens: bfloat16 [768, 39200], P('row', ('dp', 'col')), may hold values from -6 to 6
- grad_out: bfloat16 [768, 39200], P('row', ('dp', 'col')), may hold values from -6 to 6
- adapter_index: int32 [8, 1], replicated, may hold values from 0 to 7
- norm1_gain: bfloat16 [768], P('row'), may hold values from 0.099609375 to 1.8984375
- norm2_gain: bfloat16 [768], P('row'), may hold values from 0.099609375 to 1.8984375
- qkv_weight: bfloat16 [768, 2304], P('row', 'col'), may hold values from -0.21875 to 0.21875
- proj_weight: bfloat16 [768, 768], P('col', 'row'), may hold values from -0.875 to 0.875
- fc1_weight: bfloat16 [768, 3072], P('row', 'col'), may hold values from -0.21875 to 0.21875
- fc2_weight: bfloat16 [768, 3072], P('row', 'col'), may hold values from -0.109375 to 0.109375
- rel_h: bfloat16 [27, 64], replicated, may hold values from -0.59765625 to 0.59765625
- rel_w: bfloat16 [27, 64], replicated, may hold values from -0.59765625 to 0.59765625
- qkv_down: bfloat16 [8, 768, 16], P(None, 'row'), may hold values from -0.21875 to 0.21875
- qkv_up: bfloat16 [8, 16, 2304], P(None, None, 'col'), may hold values from -0.75 to 0.75
- proj_down: bfloat16 [8, 768, 16], P(None, 'col'), may hold values from -0.21875 to 0.21875
- proj_up: bfloat16 [8, 16, 768], P(None, None, 'row'), may hold values from -0.75 to 0.75
- fc1_down: bfloat16 [8, 768, 16], P(None, 'row'), may hold values from -0.21875 to 0.21875
- fc1_up: bfloat16 [8, 16, 3072], P(None, None, 'col'), may hold values from -0.75 to 0.75
- fc2_down: bfloat16 [8, 3072, 16], P(None, 'col'), may hold values from -0.109375 to 0.109375
- fc2_up: bfloat16 [8, 16, 768], P(None, None, 'row'), may hold values from -0.75 to 0.75
Outputs:
- out: bfloat16 [768, 39200], P('row', ('dp', 'col'))
- tokens_grad: float32 [768, 39200], P('row', ('dp', 'col'))
- qkv_down_grad: float32 [8, 768, 16], P(None, 'row')
- qkv_up_grad: float32 [8, 16, 2304], P(None, None, 'col')
- proj_down_grad: float32 [8, 768, 16], P(None, 'col')
- proj_up_grad: float32 [8, 16, 768], P(None, None, 'row')
- fc1_down_grad: float32 [8, 768, 16], P(None, 'row')
- fc1_up_grad: float32 [8, 16, 3072], P(None, None, 'col')
- fc2_down_grad: float32 [8, 3072, 16], P(None, 'col')
- fc2_up_grad: float32 [8, 16, 768], P(None, None, 'row')
Inputs may be any that keep to these rules, and one draw needn't show every extreme that they name: `adapter_index`: every one of the 8 adapters is chosen by at least one image.
All inputs are finite; a program needn't handle non-finite values.
Results may differ from a plain program's by a relative error of at most 0.015.
Values may be sent and summed in bfloat16 or wider, within the bound.
No kernel may reach another device: no remote copies, remote signals or barrier semaphores. Data moves between devices by JAX's collectives and lax.ppermute only.
A program may use at most 448 MiB of HBM per device.

v0:
```python
import jax
import jax.numpy as jnp
from jax import lax
from jax.sharding import PartitionSpec as P

D = 768
HD = 64
WIN = 14
SIDE = 64
ADAPT = 8
NWIN_SIDE = 5
IMG_TOK = 4900
PRECISE = lax.Precision.HIGHEST
EPSILON = 1e-06


def exact_gelu(values):
    return jax.nn.gelu(values, approximate=False)


def valid_rows():
    position = jnp.arange(IMG_TOK, dtype=jnp.int32)
    window = position // (WIN * WIN)
    inside = position % (WIN * WIN)
    image_row = window // NWIN_SIDE * WIN + inside // WIN
    image_col = window % NWIN_SIDE * WIN + inside % WIN
    return ((image_row < SIDE) & (image_col < SIDE)).astype(jnp.float32)


def rel_table(rel_param):
    offsets = (
        jnp.arange(WIN, dtype=jnp.int32)[:, None]
        - jnp.arange(WIN, dtype=jnp.int32)[None, :]
        + WIN
        - 1
    )
    one_hot = (
        offsets[:, :, None] == jnp.arange(2 * WIN - 1, dtype=jnp.int32)[None, None, :]
    ).astype(jnp.bfloat16)
    return jnp.einsum("akn,nc->akc", one_hot, rel_param, preferred_element_type=jnp.float32).astype(
        jnp.bfloat16
    )


def pick_one(adapter, own_pick):
    return jnp.einsum("a,ade->de", own_pick, adapter.astype(jnp.float32), precision=PRECISE).astype(
        jnp.bfloat16
    )


def row_totals(first_sum, second_sum):
    return lax.psum((first_sum, second_sum), "row")


def norm_forward(values):
    totals = row_totals(jnp.sum(values, axis=1), jnp.sum(values * values, axis=1))
    center = totals[0] / D
    inv_std = lax.rsqrt(totals[1] / D - center * center + EPSILON)
    return ((values - center[:, None]) * inv_std[:, None], inv_std)


def norm_backward(grad_normed, normed, inv_std):
    totals = row_totals(jnp.sum(grad_normed, axis=1), jnp.sum(grad_normed * normed, axis=1))
    return inv_std[:, None] * (
        grad_normed - totals[0][:, None] / D - normed * totals[1][:, None] / D
    )


def local_norm(values):
    center = jnp.sum(values, axis=1) / D
    inv_std = lax.rsqrt(jnp.sum(values * values, axis=1) / D - center * center + EPSILON)
    return ((values - center[:, None]) * inv_std[:, None], inv_std)


def local_norm_back(grad_normed, normed, inv_std):
    first_mean = jnp.sum(grad_normed, axis=1) / D
    second_mean = jnp.sum(grad_normed * normed, axis=1) / D
    return inv_std[:, None] * (grad_normed - first_mean[:, None] - normed * second_mean[:, None])


def to_features(values):
    return lax.all_to_all(
        values.astype(jnp.bfloat16), "row", split_axis=0, concat_axis=1, tiled=True
    ).astype(values.dtype)


def to_tokens(values):
    return lax.all_to_all(
        values.astype(jnp.bfloat16), "row", split_axis=1, concat_axis=0, tiled=True
    ).astype(values.dtype)


def token_rows(values):
    return lax.all_to_all(values, "row", split_axis=0, concat_axis=1, tiled=True)


def head_cols(values):
    return lax.all_to_all(values, "row", split_axis=1, concat_axis=0, tiled=True)


def head_sums(values):
    return lax.all_to_all(
        values.astype(jnp.bfloat16), "row", split_axis=1, concat_axis=0, tiled=True
    ).astype(values.dtype)


def adapted_local(inputs, weight, down_mat, up_mat):
    product = jnp.dot(inputs, weight, preferred_element_type=jnp.float32)
    reduced = jnp.dot(inputs, down_mat, preferred_element_type=jnp.float32)
    return product + jnp.dot(reduced, up_mat.astype(jnp.float32), precision=PRECISE)


def adapted_back(grads, weight, down_mat, up_mat):
    contract = (((1,), (1,)), ((), ()))
    product = lax.dot_general(grads, weight, contract, preferred_element_type=jnp.float32)
    reduced = lax.dot_general(grads, up_mat, contract, preferred_element_type=jnp.float32)
    return product + lax.dot_general(
        reduced, down_mat.astype(jnp.float32), contract, precision=PRECISE
    )


def pair_grads(inputs_m, grads_m, down_m, up_m):
    reduced = jnp.dot(inputs_m, down_m, preferred_element_type=jnp.float32)
    back_red = lax.dot_general(
        grads_m, up_m, (((1,), (1,)), ((), ())), preferred_element_type=jnp.float32
    )
    grad_down = jnp.einsum("td,tr->dr", inputs_m, back_red, precision=PRECISE)
    grad_up = jnp.einsum("tr,to->ro", reduced, grads_m, precision=PRECISE)
    return (grad_down, grad_up)


def spread_pick(own_pick, grad_mat):
    return jnp.einsum("a,de->ade", own_pick, grad_mat)


def take_block(full, dim, index, length):
    return lax.dynamic_slice_in_dim(full, index * length, length, dim)


def split_qkv(qkv_low):
    heads_local = qkv_low.shape[1] // (3 * HD)
    arranged = qkv_low.reshape(NWIN_SIDE * NWIN_SIDE, WIN * WIN, heads_local, 3, HD)
    return (arranged[:, :, :, 0], arranged[:, :, :, 1], arranged[:, :, :, 2])


def score_matrix(query_b, key_b, tables):
    windows = query_b.shape[0]
    heads_local = query_b.shape[2]
    dot_scores = jnp.einsum(
        "nqhc,nkhc->nhqk", query_b, key_b, preferred_element_type=jnp.float32
    ) * HD ** (-0.5)
    spatial = query_b.reshape(windows, WIN, WIN, heads_local, HD)
    rel_rows = jnp.einsum(
        "nabhc,akc->nhabk", spatial, tables[0], preferred_element_type=jnp.float32
    )
    rel_cols = jnp.einsum(
        "nabhc,bkc->nhabk", spatial, tables[1], preferred_element_type=jnp.float32
    )
    shaped = dot_scores.reshape(windows, heads_local, WIN, WIN, WIN, WIN)
    shaped = shaped + rel_rows[:, :, :, :, :, None] + rel_cols[:, :, :, :, None, :]
    return shaped.reshape(windows, heads_local, WIN * WIN, WIN * WIN)


def attend(qkv_low, tables):
    query_b, key_b, value_b = split_qkv(qkv_low)
    scores = score_matrix(query_b, key_b, tables)
    maxima = jnp.max(scores, axis=3, keepdims=True)
    exponent = jnp.exp(scores - maxima)
    sum_exp = jnp.sum(exponent, axis=3, keepdims=True)
    attn_prob = (exponent / sum_exp).astype(jnp.bfloat16)
    attended = jnp.einsum("nhqk,nkhc->nqhc", attn_prob, value_b, preferred_element_type=jnp.float32)
    log_total = (maxima + jnp.log(sum_exp))[:, :, :, 0]
    return (attended.reshape(IMG_TOK, attended.shape[2] * HD).astype(jnp.bfloat16), log_total)


def attend_back(qkv_low, log_total, grad_attended, tables):
    query_b, key_b, value_b = split_qkv(qkv_low)
    windows = query_b.shape[0]
    heads_local = query_b.shape[2]
    scores = score_matrix(query_b, key_b, tables)
    attn_exact = jnp.exp(scores - log_total[:, :, :, None])
    prob_low = attn_exact.astype(jnp.bfloat16)
    grad_o = grad_attended.reshape(windows, WIN * WIN, heads_local, HD)
    grad_v = jnp.einsum("nhqk,nqhc->nkhc", prob_low, grad_o, preferred_element_type=jnp.float32)
    grad_p = jnp.einsum("nqhc,nkhc->nhqk", grad_o, value_b, preferred_element_type=jnp.float32)
    centre = jnp.sum(grad_p * attn_exact, axis=3, keepdims=True)
    grad_s = (attn_exact * (grad_p - centre)).astype(jnp.bfloat16)
    grad_q = jnp.einsum(
        "nhqk,nkhc->nqhc", grad_s, key_b, preferred_element_type=jnp.float32
    ) * HD ** (-0.5)
    grad_k = jnp.einsum(
        "nhqk,nqhc->nkhc", grad_s, query_b, preferred_element_type=jnp.float32
    ) * HD ** (-0.5)
    split_grad = grad_s.astype(jnp.float32).reshape(windows, heads_local, WIN, WIN, WIN, WIN)
    along_rows = jnp.sum(split_grad, axis=5)
    along_cols = jnp.sum(split_grad, axis=4)
    rel_grad = jnp.einsum(
        "nhabk,akc->nabhc", along_rows, tables[0].astype(jnp.float32), precision=PRECISE
    )
    rel_grad = rel_grad + jnp.einsum(
        "nhabk,bkc->nabhc", along_cols, tables[1].astype(jnp.float32), precision=PRECISE
    )
    grad_q = grad_q + rel_grad.reshape(windows, WIN * WIN, heads_local, HD)
    stacked = jnp.stack([grad_q, grad_k, grad_v], axis=3)
    return stacked.reshape(IMG_TOK, heads_local * 3 * HD).astype(jnp.bfloat16)


def body(
    tokens,
    grad_out,
    adapter_index,
    norm1_gain,
    norm2_gain,
    qkv_weight,
    proj_weight,
    fc1_weight,
    fc2_weight,
    rel_h,
    rel_w,
    qkv_down,
    qkv_up,
    proj_down,
    proj_up,
    fc1_down,
    fc1_up,
    fc2_down,
    fc2_up,
):
    members = lax.axis_size("col")
    row_index = lax.axis_index("row")
    col_index = lax.axis_index("col")
    group_ids = lax.dynamic_slice_in_dim(
        adapter_index[:, 0], lax.axis_index("dp") * members, members, 0
    )
    chosen = (group_ids[:, None] == jnp.arange(ADAPT, dtype=jnp.int32)[None, :]).astype(jnp.float32)
    own_pick = chosen[col_index]
    validity = valid_rows()[:, None]
    tables = (rel_table(rel_h), rel_table(rel_w))
    inputs = tokens.astype(jnp.float32).T
    normed_one, inv_one = norm_forward(inputs)
    gain_one = norm1_gain.astype(jnp.float32)
    hidden_one = (normed_one * gain_one * validity).astype(jnp.bfloat16)
    qkv_part, proj_part, qkv_dn_part, proj_up_part = (
        lax.all_gather(qkv_weight, "row", axis=0, tiled=True),
        lax.all_gather(proj_weight, "row", axis=1, tiled=True),
        lax.all_gather(qkv_down, "row", axis=1, tiled=True),
        lax.all_gather(proj_up, "row", axis=2, tiled=True),
    )
    qkv_full, proj_full, qkv_up_all, proj_dn_all = (
        lax.all_gather(qkv_part, "col", axis=1, tiled=True),
        lax.all_gather(proj_part, "col", axis=0, tiled=True),
        lax.all_gather(qkv_up, "col", axis=2, tiled=True),
        lax.all_gather(proj_down, "col", axis=1, tiled=True),
    )
    qkv_dn = pick_one(qkv_dn_part, own_pick)
    qkv_upm = pick_one(qkv_up_all, own_pick)
    proj_dn = pick_one(proj_dn_all, own_pick)
    proj_upm = pick_one(proj_up_part, own_pick)
    hidden_rows = token_rows(hidden_one)
    qkv_rows_out = adapted_local(hidden_rows, qkv_full, qkv_dn, qkv_upm).astype(jnp.bfloat16)
    qkv_low = head_cols(qkv_rows_out)
    attended, log_total = attend(qkv_low, tables)
    attended_rows = token_rows(attended)
    branch = head_sums(adapted_local(attended_rows, proj_full, proj_dn, proj_upm))
    middle = inputs + branch
    grad_final = grad_out.astype(jnp.float32).T * validity
    weight_up, weight_stored, down_one, up_two, gain_full = (
        lax.all_gather(fc1_weight, "row", axis=0, tiled=True),
        lax.all_gather(fc2_weight, "row", axis=0, tiled=True),
        lax.all_gather(fc1_down, "row", axis=1, tiled=True),
        lax.all_gather(fc2_up, "row", axis=2, tiled=True),
        lax.all_gather(norm2_gain, "row", axis=0, tiled=True),
    )
    weight_up, weight_stored, up_one, down_two = (
        lax.all_gather(weight_up, "col", axis=1, tiled=True),
        lax.all_gather(weight_stored, "col", axis=1, tiled=True),
        lax.all_gather(fc1_up, "col", axis=2, tiled=True),
        lax.all_gather(fc2_down, "col", axis=1, tiled=True),
    )
    weight_down = weight_stored.T
    down_fc1 = pick_one(down_one, own_pick)
    up_fc1 = pick_one(up_one, own_pick)
    down_fc2 = pick_one(down_two, own_pick)
    up_fc2 = pick_one(up_two, own_pick)
    local_mid = to_features(middle)
    normed_two, inv_two = local_norm(local_mid)
    gain_two = gain_full.astype(jnp.float32)
    hidden_two = (normed_two * gain_two).astype(jnp.bfloat16)
    pre_act = adapted_local(hidden_two, weight_up, down_fc1, up_fc1)
    activated = exact_gelu(pre_act).astype(jnp.bfloat16)
    mlp_out = to_tokens(adapted_local(activated, weight_down, down_fc2, up_fc2))
    grad_local = to_features(grad_final).astype(jnp.bfloat16)
    grad_activ = adapted_back(grad_local, weight_down, down_fc2, up_fc2)
    gelu_value, gelu_back = jax.vjp(exact_gelu, pre_act)
    grad_pre = gelu_back(grad_activ)[0].astype(jnp.bfloat16)
    grad_hidden_two = adapted_back(grad_pre, weight_up, down_fc1, up_fc1)
    grad_middle = grad_final + to_tokens(
        local_norm_back(grad_hidden_two * gain_two, normed_two, inv_two)
    )
    fc1_local = pair_grads(hidden_two, grad_pre, down_fc1, up_fc1)
    fc2_local = pair_grads(activated, grad_local, down_fc2, up_fc2)
    summed_all = lax.psum(
        (
            spread_pick(own_pick, fc1_local[0]),
            spread_pick(own_pick, fc1_local[1]),
            spread_pick(own_pick, fc2_local[0]),
            spread_pick(own_pick, fc2_local[1]),
        ),
        ("dp", "row", "col"),
    )
    fc1_down_grad = take_block(summed_all[0], 1, row_index, fc1_down.shape[1])
    fc1_up_grad = take_block(summed_all[1], 2, col_index, fc1_up.shape[2])
    fc2_down_grad = take_block(summed_all[2], 1, col_index, fc2_down.shape[1])
    fc2_up_grad = take_block(summed_all[3], 2, row_index, fc2_up.shape[2])
    result = ((middle + mlp_out) * validity).astype(jnp.bfloat16).T
    grad_branch = grad_middle.astype(jnp.bfloat16)
    grad_branch_rows = token_rows(grad_branch)
    grad_attended = head_cols(
        adapted_back(grad_branch_rows, proj_full, proj_dn, proj_upm).astype(jnp.bfloat16)
    )
    grad_qkv = attend_back(qkv_low, log_total, grad_attended, tables)
    grad_qkv_rows = token_rows(grad_qkv)
    grad_hidden_one = head_sums(adapted_back(grad_qkv_rows, qkv_full, qkv_dn, qkv_upm))
    qkv_pair = pair_grads(hidden_rows, grad_qkv_rows, qkv_dn, qkv_upm)
    proj_pair = pair_grads(attended_rows, grad_branch_rows, proj_dn, proj_upm)
    attn_sums = lax.psum(
        (
            spread_pick(own_pick, qkv_pair[0]),
            spread_pick(own_pick, qkv_pair[1]),
            spread_pick(own_pick, proj_pair[0]),
            spread_pick(own_pick, proj_pair[1]),
        ),
        ("dp", "row", "col"),
    )
    qkv_down_grad = take_block(attn_sums[0], 1, row_index, qkv_down.shape[1])
    qkv_up_grad = take_block(attn_sums[1], 2, col_index, qkv_up.shape[2])
    proj_down_grad = take_block(attn_sums[2], 1, col_index, proj_down.shape[1])
    proj_up_grad = take_block(attn_sums[3], 2, row_index, proj_up.shape[2])
    grad_inputs = (
        grad_middle + norm_backward(grad_hidden_one * validity * gain_one, normed_one, inv_one)
    ).T
    return (
        result,
        grad_inputs,
        qkv_down_grad,
        qkv_up_grad,
        proj_down_grad,
        proj_up_grad,
        fc1_down_grad,
        fc1_up_grad,
        fc2_down_grad,
        fc2_up_grad,
    )


def solution(mesh):
    return jax.shard_map(
        body,
        mesh=mesh,
        in_specs=(
            P("row", ("dp", "col")),
            P("row", ("dp", "col")),
            P(),
            P("row"),
            P("row"),
            P("row", "col"),
            P("col", "row"),
            P("row", "col"),
            P("row", "col"),
            P(),
            P(),
            P(None, "row", None),
            P(None, None, "col"),
            P(None, "col", None),
            P(None, None, "row"),
            P(None, "row", None),
            P(None, None, "col"),
            P(None, "col", None),
            P(None, None, "row"),
        ),
        out_specs=(
            P("row", ("dp", "col")),
            P("row", ("dp", "col")),
            P(None, "row", None),
            P(None, None, "col"),
            P(None, "col", None),
            P(None, None, "row"),
            P(None, "row", None),
            P(None, None, "col"),
            P(None, "col", None),
            P(None, None, "row"),
        ),
        check_vma=False,
    )
```

profile of v0, /device:TPU:0, one launch (start us, length us, event | category | flops | bytes accessed | tf_op | source)
XLA Modules:
  0.0 1826.9 jit_solution(15166732212104624496)
XLA Ops:
  46.7 118.0 %all_gather.54 = bf16[8,16,2304]{1,0,2:T(8,128)(2,1)} all-gather(bf16[8,16,576]{1,0,2:T(8,128)(2,1)S(1)} %copy.225), channel_id=1, replica_groups=mesh['dp'=2,'row'=4,'col'=4] {'col'}, dimensions={2}, use_global_device_ids=true | all-gather | bytes 737280 | tf_op jit(solution)/shard_map/all_gather | solution.py:252
  184.5 30.9 %all_gather.57 = bf16[8,768,16]{2,0,1:T(8,128)(2,1)S(1)} all-gather(bf16[8,192,16]{2,0,1:T(8,128)(2,1)} %copy.243), channel_id=1, replica_groups=mesh['dp'=2,'row'=4,'col'=4] {'col'}, dimensions={1}, use_global_device_ids=true | all-gather | bytes 245760 | tf_op jit(solution)/shard_map/all_gather | solution.py:253
  263.0 74.5 %all_gather.55 = bf16[192,768]{0,1:T(8,128)(2,1)S(1)} all-gather(bf16[192,192]{0,1:T(8,128)(2,1)S(1)} %copy.241), channel_id=1, replica_groups=mesh['dp'=2,'row'=4,'col'=4] {'row'}, dimensions={1}, use_global_device_ids=true | all-gather | bytes 368640 | tf_op jit(solution)/shard_map/all_gather | solution.py:245
  372.0 26.8 %reshape.211 = bf16[25,196,3,3,64]{1,0,4,3,2:T(8,128)(2,1)} reshape(bf16[4,1225,576]{1,0,2:T(4,128)(2,1)} %copy.227) | data formatting | bytes 11289600 | tf_op jit(solution)/shard_map/reshape | solution.py:142
  427.1 21.4 %add.271 = f32[25,3,14,14,14,14]{0,5,4,3,2,1:T(8,128)} broadcast(f32[25,3,14,14,14]{0,4,3,2,1:T(8,128)S(1)} %copy.236), dimensions={0,1,2,3,5} | broadcast | bytes 12348000 | tf_op jit(solution)/shard_map/add | solution.py:160
  448.6 64.5 %add.272 = f32[25,3,196,196]{0,3,2,1:T(8,128)} reshape(f32[25,3,14,14,14,14]{0,5,4,3,2,1:T(8,128)} %add.271) | data formatting | bytes 23049600 | tf_op jit(solution)/shard_map/add | solution.py:160
  513.1 39.1 %copy.237 = f32[25,3,196,196]{2,3,1,0:T(8,128)} copy(f32[25,3,196,196]{0,3,2,1:T(8,128)} %add.272) | data formatting | bytes 23049600 | tf_op jit(solution)/shard_map/add | solution.py:160
  563.4 22.8 %add.268 = f32[25,3,14,14,14,14]{0,5,4,3,2,1:T(8,128)} broadcast(f32[25,3,14,14,14]{0,4,3,2,1:T(8,128)} %copy.233), dimensions={0,1,2,3,4} | broadcast | bytes 12348000 | tf_op jit(solution)/shard_map/add | solution.py:160
  586.3 64.5 %add.269 = f32[25,3,196,196]{0,3,2,1:T(8,128)} reshape(f32[25,3,14,14,14,14]{0,5,4,3,2,1:T(8,128)} %add.268) | data formatting | bytes 23049600 | tf_op jit(solution)/shard_map/add | solution.py:160
  650.8 39.1 %copy.234 = f32[25,3,196,196]{2,3,1,0:T(8,128)} copy(f32[25,3,196,196]{0,3,2,1:T(8,128)} %add.269) | data formatting | bytes 23049600 | tf_op jit(solution)/shard_map/add | solution.py:160
  689.9 24.5 %fusion.132 = (f32[25,3,196]{2,1,0:T(4,128)S(1)}, f32[25,3,196,196]{2,3,1,0:T(8,128)}) fusion(f32[25,3,196,196]{2,3,1,0:T(8,128)} %copy.237, f32[25,3,196,196]{2,3,1,0:T(8,128)} %copy.234, bf16[25,196,3,1,64]{1,0,4,3,2:T(8,128)(2,1)} %get-tuple-element.37, bf16[25,196,3,1,64]{1,0,4,3,2:T(8,128)(2,1)S(1)} %copy-done.9), kind=kOutput, calls=%fused_computation.234 | convolution fusion | flops 380303744 | bytes 38396400 | tf_op jit(solution)/shard_map/nqhc,nkhc->nhqk/dot_general | solution.py:149
  779.3 33.6 %all_gather.67 = bf16[8,16,768]{1,0,2:T(8,128)(2,1)S(1)} all-gather(bf16[8,16,192]{1,0,2:T(8,128)(2,1)} %copy.250), channel_id=1, replica_groups=mesh['dp'=2,'row'=4,'col'=4] {'row'}, dimensions={2}, use_global_device_ids=true | all-gather | bytes 245760 | tf_op jit(solution)/shard_map/all_gather | solution.py:271
  868.1 30.2 %all_gather.63 = bf16[8,16,3072]{2,1,0:T(8,128)(2,1)S(1)} all-gather(bf16[8,16,768]{2,1,0:T(8,128)(2,1)S(1)} %copy-done.72), channel_id=1, replica_groups=mesh['dp'=2,'row'=4,'col'=4] {'col'}, dimensions={2}, use_global_device_ids=true | all-gather | bytes 983040 | tf_op jit(solution)/shard_map/all_gather | solution.py:277
  975.9 41.4 %multiply_convert_fusion.1 = (bf16[1225,3072]{1,0:T(8,128)(2,1)}, f32[1225,3072]{1,0:T(8,128)}, f32[1225,3072]{1,0:T(8,128)}) fusion(f32[1225,3072]{1,0:T(8,128)S(1)} %fusion.135, f32[1225,16]{0,1:T(8,128)S(1)} %fusion.149, bf16[1,16,3072]{2,0,1:T(2,128)(2,1)S(1)} %fusion.64), kind=kOutput, calls=%fused_computation.9 | convolution fusion | flops 970905600 | bytes 52861504 | tf_op jit(solution)/shard_map/dot_general | solution.py:110
  1017.3 23.1 %add_convert_fusion = bf16[1225,3072]{1,0:T(8,128)(2,1)} fusion(f32[1225,3072]{1,0:T(8,128)} %get-tuple-element.32, f32[1225,3072]{1,0:T(8,128)} %fusion.137, f32[1225,3072]{1,0:T(8,128)} %get-tuple-element.51, f32[1225,16]{0,1:T(8,128)S(1)} %fusion.116, bf16[1,3072,16]{1,2,0:T(8,128)(2,1)S(1)} %copy.292), kind=kOutput, calls=%fused_computation.8 | convolution fusion | flops 778982400 | bytes 52861504 | tf_op jit(solution)/shard_map/dot_general | solution.py:117
  1062.8 26.9 %all_to_all.186 = bf16[1225,4,192]{0,2,1:T(8,128)(2,1)S(1)} all-to-all(bf16[1225,4,192]{0,2,1:T(8,128)(2,1)S(1)} %bitcast.307), channel_id=1, replica_groups=mesh['dp'=2,'row'=4,'col'=4] {'row'}, dimensions={1} | all-to-all | bytes 3763200 | tf_op jit(solution)/shard_map/all_to_all | solution.py:88
  1114.9 23.5 %all-to-all-done.8 = bf16[4,1225,192]{1,2,0:T(8,128)(2,1)S(1)} async-done(((bf16[4,1225,192]{1,2,0:T(8,128)(2,1)}), bf16[4,1225,192]{1,2,0:T(8,128)(2,1)S(1)}, u32[]{:S(2)}, u32[]{:S(2)}) %all-to-all-start.8) | async-done | bytes 1881632 | tf_op jit(solution)/shard_map/all_to_all | solution.py:94
  1208.2 21.7 %multiply_reduce_fusion = (f32[25,3,196]{2,1,0:T(4,128)S(1)}, f32[25,3,196,196]{2,3,1,0:T(8,128)}) fusion(f32[25,3,196,196]{2,3,1,0:T(8,128)} %get-tuple-element.50, f32[25,3,196]{2,1,0:T(4,128)S(1)} %log_add_fusion, bf16[25,196,3,1,64]{1,0,4,3,2:T(8,128)(2,1)} %get-tuple-element.35, bf16[25,196,3,64]{1,0,3,2:T(8,128)(2,1)S(1)} %reshape.212), kind=kOutput, calls=%fused_computation.2 | convolution fusion | flops 377422528 | bytes 26930400 | tf_op jit(solution)/shard_map/nqhc,nkhc->nhqk/dot_general | solution.py:185
  1249.0 30.3 %copy.261 = f32[25,3,196,196]{0,3,2,1:T(8,128)} copy(bf16[25,3,196,196]{2,3,1,0:T(8,128)(2,1)} %copy-done.2) | data formatting | bytes 17287200 | tf_op jit(solution)/shard_map/reshape | solution.py:194
  1279.4 64.6 %reshape.221 = f32[25,3,14,14,14,14]{0,5,4,3,2,1:T(8,128)} reshape(f32[25,3,196,196]{0,3,2,1:T(8,128)} %copy.261) | data formatting | bytes 23049600 | tf_op jit(solution)/shard_map/reshape | solution.py:194
  1344.0 94.7 %fusion.128 = (f32[25,3,14,14,14]{0,4,3,2,1:T(8,128)}, f32[25,3,14,14,14]{0,4,3,2,1:T(8,128)}) fusion(f32[25,3,14,14,14,14]{0,5,4,3,2,1:T(8,128)} %reshape.221), kind=kLoop, calls=%fused_computation.231 | loop fusion | flops 5350800 | bytes 13171200 | tf_op jit(solution)/shard_map/reduce_sum | solution.py:195
  1506.5 24.2 %convert_element_type.249 = bf16[4,1225,576]{1,0,2:T(4,128)(2,1)} reshape(bf16[25,196,3,3,64]{1,0,4,3,2:T(8,128)(2,1)} %copy.269) | data formatting | bytes 11289600 | tf_op jit(solution)/shard_map/convert_element_type | solution.py:205
  1577.8 31.0 %all-to-all-done.10 = bf16[4,1225,576]{1,2,0:T(8,128)(2,1)} async-done(((bf16[4,1225,576]{1,2,0:T(8,128)(2,1)}), bf16[4,1225,576]{1,2,0:T(8,128)(2,1)}, u32[]{:S(2)}, u32[]{:S(2)}) %all-to-all-start.10) | async-done | bytes 5644832 | tf_op jit(solution)/shard_map/all_to_all | solution.py:94
  1699.4 106.6 %all-reduce.6.cloned.1.call-done = (f32[8,768,16]{1,2,0:T(8,128)}, f32[8,16,2304]{2,1,0:T(8,128)}, f32[8,768,16]{1,2,0:T(8,128)}, f32[8,16,768]{2,1,0:T(8,128)},...) async-done(((f32[8,768,16]{1,2,0:T(8,128)}, f32[8,16,2304]{2,1,0:T(8,128)}, f32[8,768,16]{1,2,0:T(8,128)}, ...) | async-done | bytes 6291472 | tf_op jit(solution)/shard_map/psum | solution.py:326
  (394 shorter events, 732.5 us)
Async XLA Ops:
  7.2 354.6 %copy-start = (bf16[27,64]{1,0:T(8,128)(2,1)S(1)}, bf16[27,64]{1,0:T(8,128)(2,1)}, u32[]{:S(2)}) copy-start(bf16[27,64]{1,0:T(8,128)(2,1)} %param.28) | copy-start | bytes 10372
  7.2 225.9 %all-gather.7.cloned.1.call-start = ((), (), s32[]{:S(2)}) async-start(), calls=%async_computation.12 | async-start | bytes 4423680 | tf_op jit(solution)/shard_map/all_gather | solution.py:250
  41.5 191.2 %all-to-all-start = ((bf16[4,1225,192]{1,2,0:T(8,128)(2,1)}), bf16[4,1225,192]{1,2,0:T(8,128)(2,1)S(1)}, u32[]{:S(2)}, u32[]{:S(2)}) async-start(bf16[4,1225,192]{1,2,0:T(8,128)(2,1)} %copy.222), calls=%async_computation | async-start | bytes 3932160 | tf_op jit(solution)/shard_map/all_to_all | solution.py:94
  45.1 119.6 %copy-start.76 = (bf16[8,192,16]{1,2,0:T(8,128)(2,1)S(1)}, bf16[8,192,16]{1,2,0:T(8,128)(2,1)}, u32[]{:S(2)}) copy-start(bf16[8,192,16]{1,2,0:T(8,128)(2,1)} %param.34) | copy-start | bytes 147460
  45.1 317.2 %all-gather.15.cloned.1.call-start = ((), (), s32[]{:S(2)}) async-start(), calls=%async_computation.16 | async-start | bytes 1474560 | tf_op jit(solution)/shard_map/all_gather | solution.py:269
  45.9 120.1 %copy-start.78 = (bf16[8,192,16]{1,2,0:T(8,128)(2,1)S(1)}, bf16[8,192,16]{1,2,0:T(8,128)(2,1)}, u32[]{:S(2)}) copy-start(bf16[8,192,16]{1,2,0:T(8,128)(2,1)} %param.30) | copy-start | bytes 147460
  256.5 105.8 %all-to-all-start.1 = ((bf16[1225,4,576]{0,2,1:T(8,128)(2,1)}), bf16[1225,4,576]{0,2,1:T(8,128)(2,1)}, u32[]{:S(2)}, u32[]{:S(2)}) async-start(bf16[1225,4,576]{0,2,1:T(8,128)(2,1)} %bitcast.293), calls=%async_computation.1 | async-start | bytes 11796480 | tf_op jit(solution)/shard_map/all_to_all | solution.py:98
  261.9 572.0 %all-gather.11.cloned.1.call-start = ((), (), s32[]{:S(2)}) async-start(), calls=%async_computation.14 | async-start | bytes 1474560 | tf_op jit(solution)/shard_map/all_gather | solution.py:268
  262.6 571.3 %all-gather.9.cloned.1.call-start = ((), (), s32[]{:S(2)}) async-start(), calls=%async_computation.13 | async-start | bytes 1474560 | tf_op jit(solution)/shard_map/all_gather | solution.py:251
  338.4 590.4 %all-gather.17.cloned.1.call-start = ((), (), s32[]{:S(2)}) async-start(), calls=%async_computation.17 | async-start | bytes 5898240 | tf_op jit(solution)/shard_map/all_gather | solution.py:276
  362.0 190.1 %copy-start.63 = (bf16[14,14,64,1,1]{2,1,4,3,0:T(8,128)(2,1)}, bf16[14,14,64,1,1]{2,1,4,3,0:T(8,128)(2,1)S(1)}, u32[]{:S(2)}) copy-start(bf16[14,14,64,1,1]{2,1,4,3,0:T(8,128)(2,1)S(1)} %fusion.61) | copy-start | bytes 75268
  746.5 27.9 %all-to-all-start.2 = ((bf16[4,1225,192]{1,2,0:T(8,128)(2,1)}), bf16[4,1225,192]{1,2,0:T(8,128)(2,1)S(1)}, u32[]{:S(2)}, u32[]{:S(2)}) async-start(bf16[4,1225,192]{1,2,0:T(8,128)(2,1)} %copy.240), calls=%async_computation.2 | async-start | bytes 3932160 | tf_op jit(solution)/shard_map/all_to_all | solution.py:94
  775.7 70.0 %all-to-all-start.6 = ((bf16[4,1225,192]{1,2,0:T(8,128)(2,1)}), bf16[4,1225,192]{1,2,0:T(8,128)(2,1)S(1)}, u32[]{:S(2)}, u32[]{:S(2)}) async-start(bf16[4,1225,192]{1,2,0:T(8,128)(2,1)} %copy.253), calls=%async_computation.6 | async-start | bytes 3932160 | tf_op jit(solution)/shard_map/all_to_all | solution.py:82
  779.3 188.6 %all-gather.13.cloned.1.call-start = ((), (), s32[]{:S(2)}) async-start(), calls=%async_computation.15 | async-start | bytes 5898240 | tf_op jit(solution)/shard_map/all_gather | solution.py:275
  845.7 53.6 %all-to-all-start.3 = ((bf16[1225,4,192]{0,2,1:T(8,128)(2,1)}), bf16[1225,4,192]{0,2,1:T(8,128)(2,1)}, u32[]{:S(2)}, u32[]{:S(2)}) async-start(bf16[1225,4,192]{0,2,1:T(8,128)(2,1)} %bitcast.305), calls=%async_computation.3 | async-start | bytes 3932160 | tf_op jit(solution)/shard_map/all_to_all | solution.py:102
  867.8 149.5 %copy-start.55 = (bf16[1,3072,16]{1,2,0:T(8,128)(2,1)}, bf16[1,3072,16]{1,2,0:T(8,128)(2,1)S(1)}, u32[]{:S(2)}) copy-start(bf16[1,3072,16]{1,2,0:T(8,128)(2,1)S(1)} %copy.292) | copy-start | bytes 294916
  924.1 29.0 %all-to-all-start.4 = ((bf16[4,1225,192]{1,2,0:T(8,128)(2,1)}), bf16[4,1225,192]{1,2,0:T(8,128)(2,1)}, u32[]{:S(2)}, u32[]{:S(2)}) async-start(bf16[4,1225,192]{1,2,0:T(8,128)(2,1)} %copy.247), calls=%async_computation.4 | async-start | bytes 3932160 | tf_op jit(solution)/shard_map/all_to_all | solution.py:82
  1110.5 27.9 %all-to-all-start.8 = ((bf16[4,1225,192]{1,2,0:T(8,128)(2,1)}), bf16[4,1225,192]{1,2,0:T(8,128)(2,1)S(1)}, u32[]{:S(2)}, u32[]{:S(2)}) async-start(bf16[4,1225,192]{1,2,0:T(8,128)(2,1)} %copy.256), calls=%async_computation.8 | async-start | bytes 3932160 | tf_op jit(solution)/shard_map/all_to_all | solution.py:94
  1149.2 29.3 %all-to-all-start.9 = ((bf16[1225,4,192]{0,2,1:T(8,128)(2,1)}), bf16[1225,4,192]{0,2,1:T(8,128)(2,1)}, u32[]{:S(2)}, u32[]{:S(2)}) async-start(bf16[1225,4,192]{0,2,1:T(8,128)(2,1)} %bitcast.306), calls=%async_computation.9 | async-start | bytes 3932160 | tf_op jit(solution)/shard_map/all_to_all | solution.py:98
  1178.5 358.2 %all-to-all-start.5 = ((bf16[1225,4,192]{0,2,1:T(8,128)(2,1)}), bf16[1225,4,192]{0,2,1:T(8,128)(2,1)}, u32[]{:S(2)}, u32[]{:S(2)}) async-start(bf16[1225,4,192]{0,2,1:T(8,128)(2,1)} %bitcast.38), calls=%async_computation.5 | async-start | bytes 3932160 | tf_op jit(solution)/shard_map/all_to_all | solution.py:88
  1536.7 72.1 %all-to-all-start.10 = ((bf16[4,1225,576]{1,2,0:T(8,128)(2,1)}), bf16[4,1225,576]{1,2,0:T(8,128)(2,1)}, u32[]{:S(2)}, u32[]{:S(2)}) async-start(bf16[4,1225,576]{1,2,0:T(8,128)(2,1)} %copy.270), calls=%async_computation.10 | async-start | bytes 11796480 | tf_op jit(solution)/shard_map/all_to_all | solution.py:94
  1627.2 33.6 %all-to-all-start.11 = ((bf16[1225,4,192]{0,2,1:T(8,128)(2,1)}), bf16[1225,4,192]{0,2,1:T(8,128)(2,1)}, u32[]{:S(2)}, u32[]{:S(2)}) async-start(bf16[1225,4,192]{0,2,1:T(8,128)(2,1)} %bitcast.304), calls=%async_computation.11 | async-start | bytes 3932160 | tf_op jit(solution)/shard_map/all_to_all | solution.py:102
  1631.8 174.2 %all-reduce.6.cloned.1.call-start = ((), (), s32[]{:S(2)}) async-start(), calls=%async_computation.18 | async-start | bytes 12582912 | tf_op jit(solution)/shard_map/psum | solution.py:326
  1689.6 130.2 %copy-start.1 = (bf16[27,64]{1,0:T(8,128)(2,1)S(1)}, bf16[27,64]{1,0:T(8,128)(2,1)}, u32[]{:S(2)}) copy-start(bf16[27,64]{1,0:T(8,128)(2,1)} %param.28) | copy-start | bytes 10372
  (92 other events, 1562.8 us)
Sparse Core Ops, SparseCore 0:
  20.2 108.6 all-gather.6
  130.5 16.0 all-gather.14
  264.3 24.6 all-gather.10
  338.5 29.8 all-gather.8
  369.8 88.5 all-gather.16
  834.0 100.3 all-gather.12
  1643.3 162.6 all-reduce.5
where the time goes:
time: 1840 us; the launch traced here: 1830 us
  local copies, waits for them, and re-layouts  647 us (35%)
  blocking collectives  412 us (22%)
  matrix products  314 us (17%)
  waiting for transfers between devices  211 us (11%)
  other arithmetic  177 us (10%)
  starting transfers between devices  49.4 us (3%)
    add x6, local copies, waits for them, and re-layouts, score_matrix(): shaped + rel_rows[:, :, :, :, :, None] + rel_cols[:, :, :, :, None, :]  251 us
    all_gather x1, blocking collectives, body(): lax.all_gather(qkv_up, 'col', axis=2, tiled=True)  118 us
    psum x1, waiting for transfers between devices, body(): lax.psum((spread_pick(own_pick, qkv_pair[0]), spread_pick(own_pick, qkv_p...  107 us
    reshape x2, local copies, waits for them, and re-layouts, attend_back(): grad_s.astype(jnp.float32).reshape(windows, heads_local, WIN, WIN, WIN, WIN)  94.9 us
    reduce_sum x1, other arithmetic, attend_back(): along_rows = jnp.sum(split_grad, axis=5)  94.7 us
    all_gather x1, blocking collectives, body(): lax.all_gather(proj_weight, 'row', axis=1, tiled=True)  74.5 us
    all_to_all x4, waiting for transfers between devices, token_rows(): lax.all_to_all(values, 'row', split_axis=0, concat_axis=1, tiled=True)  65.1 us
    dot_general x4, matrix products, adapted_local(): jnp.dot(reduced, up_mat.astype(jnp.float32), precision=PRECISE)  53.4 us
  transfers between devices with their start and end apart: 18, of which 7 were waited for; matrix products, arithmetic and copies ran while one was open for 52% of the time, Pallas kernels for 0%

commit v1 on v0

--- a/solution.py
+++ b/solution.py
@@ -12,6 +12,19 @@
 IMG_TOK = 4900
 PRECISE = lax.Precision.HIGHEST
 EPSILON = 1e-06
+
+
+def gather_around(array, axis, dim):
+    ways = lax.axis_size(axis)
+    up = [(d, (d + 1) % ways) for d in range(ways)]
+    down = [(d, (d - 1) % ways) for d in range(ways)]
+    earlier, later = ([array], [array])
+    for _ in range(ways // 2):
+        earlier.append(lax.ppermute(earlier[-1], axis, up))
+    for _ in range((ways - 1) // 2):
+        later.append(lax.ppermute(later[-1], axis, down))
+    line = jnp.concatenate([*earlier[::-1], *later[1:]], axis=dim)
+    return jnp.roll(line, (lax.axis_index(axis) - ways // 2) * array.shape[dim], axis=dim)
 
 
 def exact_gelu(values):
@@ -249,7 +262,7 @@
     qkv_full, proj_full, qkv_up_all, proj_dn_all = (
         lax.all_gather(qkv_part, "col", axis=1, tiled=True),
         lax.all_gather(proj_part, "col", axis=0, tiled=True),
-        lax.all_gather(qkv_up, "col", axis=2, tiled=True),
+        gather_around(qkv_up, "col", 2),
         lax.all_gather(proj_down, "col", axis=1, tiled=True),
     )
     qkv_dn = pick_one(qkv_dn_part, own_pick)

time: 1840 us -> 1760 us (0.957)
  blocking collectives: 412 us -> 317 us
    all_gather x1 -> x0, blocking collectives: 118 us -> none  [body(): lax.all_gather(qkv_up, 'col', axis=2, tiled=True)]
    all_gather x1, blocking collectives: 12.9 us -> 31.9 us  [body(): lax.all_gather(fc1_down, 'row', axis=1, tiled=True)]
  transfers between devices with their start and end apart: 18 -> 21, of which waited for: 7 -> 8; matrix products, arithmetic and copies ran while one was open for 52% -> 55% of each run, Pallas kernels for 0% -> 0%
where the time goes in v1:
time: 1760 us; the launch traced here: 1740 us
  local copies, waits for them, and re-layouts  647 us (37%)
  blocking collectives  317 us (18%)
  matrix products  314 us (18%)
  waiting for transfers between devices  213 us (12%)
  other arithmetic  179 us (10%)
  starting transfers between devices  54 us (3%)
    add x6, local copies, waits for them, and re-layouts, score_matrix(): shaped + rel_rows[:, :, :, :, :, None] + rel_cols[:, :, :, :, None, :]  251 us
    psum x1, waiting for transfers between devices, body(): lax.psum((spread_pick(own_pick, qkv_pair[0]), spread_pick(own_pick, qkv_p...  107 us
    reshape x2, local copies, waits for them, and re-layouts, attend_back(): grad_s.astype(jnp.float32).reshape(windows, heads_local, WIN, WIN, WIN, WIN)  94.9 us
    reduce_sum x1, other arithmetic, attend_back(): along_rows = jnp.sum(split_grad, axis=5)  94.7 us
    all_gather x1, blocking collectives, body(): lax.all_gather(proj_weight, 'row', axis=1, tiled=True)  74.7 us
    all_to_all x4, waiting for transfers between devices, token_rows(): lax.all_to_all(values, 'row', split_axis=0, concat_axis=1, tiled=True)  65.1 us
    dot_general x4, matrix products, adapted_local(): jnp.dot(reduced, up_mat.astype(jnp.float32), precision=PRECISE)  53.4 us
  transfers between devices with their start and end apart: 21, of which 8 were waited for; matrix products, arithmetic and copies ran while one was open for 55% of the time, Pallas kernels for 0%

profile of v1, /device:TPU:0, one launch (start us, length us, event | category | flops | bytes accessed | tf_op | source)
XLA Modules:
  0.0 1740.0 jit_solution(5098488279250587304)
XLA Ops:
  51.2 31.9 %all_gather.58 = bf16[8,768,16]{2,0,1:T(8,128)(2,1)S(1)} all-gather(bf16[8,192,16]{2,0,1:T(8,128)(2,1)} %copy.246), channel_id=1, replica_groups=mesh['dp'=2,'row'=4,'col'=4] {'row'}, dimensions={1}, use_global_device_ids=true | all-gather | bytes 245760 | tf_op jit(solution)/shard_map/all_gather | solution.py:283
  84.9 32.4 %all_gather.53 = bf16[8,768,16]{2,0,1:T(8,128)(2,1)} all-gather(bf16[8,192,16]{2,0,1:T(8,128)(2,1)} %copy.240), channel_id=1, replica_groups=mesh['dp'=2,'row'=4,'col'=4] {'col'}, dimensions={1}, use_global_device_ids=true | all-gather | bytes 245760 | tf_op jit(solution)/shard_map/all_gather | solution.py:266
  177.1 74.7 %all_gather.51 = bf16[192,768]{0,1:T(8,128)(2,1)S(1)} all-gather(bf16[192,192]{0,1:T(8,128)(2,1)S(1)} %copy.238), channel_id=1, replica_groups=mesh['dp'=2,'row'=4,'col'=4] {'row'}, dimensions={1}, use_global_device_ids=true | all-gather | bytes 368640 | tf_op jit(solution)/shard_map/all_gather | solution.py:258
  286.4 26.8 %reshape.211 = bf16[25,196,3,3,64]{1,0,4,3,2:T(8,128)(2,1)} reshape(bf16[4,1225,576]{1,0,2:T(4,128)(2,1)} %copy.224) | data formatting | bytes 11289600 | tf_op jit(solution)/shard_map/reshape | solution.py:155
  341.5 21.4 %add.284 = f32[25,3,14,14,14,14]{0,5,4,3,2,1:T(8,128)} broadcast(f32[25,3,14,14,14]{0,4,3,2,1:T(8,128)S(1)} %copy.233), dimensions={0,1,2,3,5} | broadcast | bytes 12348000 | tf_op jit(solution)/shard_map/add | solution.py:173
  362.9 64.5 %add.285 = f32[25,3,196,196]{0,3,2,1:T(8,128)} reshape(f32[25,3,14,14,14,14]{0,5,4,3,2,1:T(8,128)} %add.284) | data formatting | bytes 23049600 | tf_op jit(solution)/shard_map/add | solution.py:173
  427.4 39.1 %copy.234 = f32[25,3,196,196]{2,3,1,0:T(8,128)} copy(f32[25,3,196,196]{0,3,2,1:T(8,128)} %add.285) | data formatting | bytes 23049600 | tf_op jit(solution)/shard_map/add | solution.py:173
  477.8 22.8 %add.281 = f32[25,3,14,14,14,14]{0,5,4,3,2,1:T(8,128)} broadcast(f32[25,3,14,14,14]{0,4,3,2,1:T(8,128)} %copy.230), dimensions={0,1,2,3,4} | broadcast | bytes 12348000 | tf_op jit(solution)/shard_map/add | solution.py:173
  500.6 64.5 %add.282 = f32[25,3,196,196]{0,3,2,1:T(8,128)} reshape(f32[25,3,14,14,14,14]{0,5,4,3,2,1:T(8,128)} %add.281) | data formatting | bytes 23049600 | tf_op jit(solution)/shard_map/add | solution.py:173
  565.1 39.1 %copy.231 = f32[25,3,196,196]{2,3,1,0:T(8,128)} copy(f32[25,3,196,196]{0,3,2,1:T(8,128)} %add.282) | data formatting | bytes 23049600 | tf_op jit(solution)/shard_map/add | solution.py:173
  604.2 24.5 %fusion.133 = (f32[25,3,196]{2,1,0:T(4,128)S(1)}, f32[25,3,196,196]{2,3,1,0:T(8,128)}) fusion(f32[25,3,196,196]{2,3,1,0:T(8,128)} %copy.234, f32[25,3,196,196]{2,3,1,0:T(8,128)} %copy.231, bf16[25,196,3,1,64]{1,0,4,3,2:T(8,128)(2,1)} %get-tuple-element.37, bf16[25,196,3,1,64]{1,0,4,3,2:T(8,128)(2,1)S(1)} %copy-done.9), kind=kOutput, calls=%fused_computation.236 | convolution fusion | flops 380303744 | bytes 38396400 | tf_op jit(solution)/shard_map/nqhc,nkhc->nhqk/dot_general | solution.py:162
  693.7 33.6 %all_gather.63 = bf16[8,16,768]{1,0,2:T(8,128)(2,1)S(1)} all-gather(bf16[8,16,192]{1,0,2:T(8,128)(2,1)} %copy.247), channel_id=1, replica_groups=mesh['dp'=2,'row'=4,'col'=4] {'row'}, dimensions={2}, use_global_device_ids=true | all-gather | bytes 245760 | tf_op jit(solution)/shard_map/all_gather | solution.py:284
  781.2 30.2 %all_gather.59 = bf16[8,16,3072]{2,1,0:T(8,128)(2,1)S(1)} all-gather(bf16[8,16,768]{2,1,0:T(8,128)(2,1)S(1)} %copy-done.72), channel_id=1, replica_groups=mesh['dp'=2,'row'=4,'col'=4] {'col'}, dimensions={2}, use_global_device_ids=true | all-gather | bytes 983040 | tf_op jit(solution)/shard_map/all_gather | solution.py:290
  889.1 41.4 %multiply_convert_fusion.1 = (bf16[1225,3072]{1,0:T(8,128)(2,1)}, f32[1225,3072]{1,0:T(8,128)}, f32[1225,3072]{1,0:T(8,128)}) fusion(f32[1225,3072]{1,0:T(8,128)S(1)} %fusion.136, f32[1225,16]{0,1:T(8,128)S(1)} %fusion.150, bf16[1,16,3072]{2,0,1:T(2,128)(2,1)S(1)} %fusion.64), kind=kOutput, calls=%fused_computation.9 | convolution fusion | flops 970905600 | bytes 52861504 | tf_op jit(solution)/shard_map/dot_general | solution.py:123
  930.5 23.1 %add_convert_fusion = bf16[1225,3072]{1,0:T(8,128)(2,1)} fusion(f32[1225,3072]{1,0:T(8,128)} %get-tuple-element.32, f32[1225,3072]{1,0:T(8,128)} %fusion.138, f32[1225,3072]{1,0:T(8,128)} %get-tuple-element.51, f32[1225,16]{0,1:T(8,128)S(1)} %fusion.118, bf16[1,3072,16]{1,2,0:T(8,128)(2,1)S(1)} %copy.289), kind=kOutput, calls=%fused_computation.8 | convolution fusion | flops 778982400 | bytes 52861504 | tf_op jit(solution)/shard_map/dot_general | solution.py:130
  975.9 26.9 %all_to_all.186 = bf16[1225,4,192]{0,2,1:T(8,128)(2,1)S(1)} all-to-all(bf16[1225,4,192]{0,2,1:T(8,128)(2,1)S(1)} %bitcast.306), channel_id=1, replica_groups=mesh['dp'=2,'row'=4,'col'=4] {'row'}, dimensions={1} | all-to-all | bytes 3763200 | tf_op jit(solution)/shard_map/all_to_all | solution.py:101
  1028.1 23.5 %all-to-all-done.8 = bf16[4,1225,192]{1,2,0:T(8,128)(2,1)S(1)} async-done(((bf16[4,1225,192]{1,2,0:T(8,128)(2,1)}), bf16[4,1225,192]{1,2,0:T(8,128)(2,1)S(1)}, u32[]{:S(2)}, u32[]{:S(2)}) %all-to-all-start.8) | async-done | bytes 1881632 | tf_op jit(solution)/shard_map/all_to_all | solution.py:107
  1121.4 21.7 %multiply_reduce_fusion = (f32[25,3,196]{2,1,0:T(4,128)S(1)}, f32[25,3,196,196]{2,3,1,0:T(8,128)}) fusion(f32[25,3,196,196]{2,3,1,0:T(8,128)} %get-tuple-element.50, f32[25,3,196]{2,1,0:T(4,128)S(1)} %log_add_fusion, bf16[25,196,3,1,64]{1,0,4,3,2:T(8,128)(2,1)} %get-tuple-element.35, bf16[25,196,3,64]{1,0,3,2:T(8,128)(2,1)S(1)} %reshape.212), kind=kOutput, calls=%fused_computation.2 | convolution fusion | flops 377422528 | bytes 26930400 | tf_op jit(solution)/shard_map/nqhc,nkhc->nhqk/dot_general | solution.py:198
  1162.2 30.3 %copy.258 = f32[25,3,196,196]{0,3,2,1:T(8,128)} copy(bf16[25,3,196,196]{2,3,1,0:T(8,128)(2,1)} %copy-done.2) | data formatting | bytes 17287200 | tf_op jit(solution)/shard_map/reshape | solution.py:207
  1192.5 64.6 %reshape.221 = f32[25,3,14,14,14,14]{0,5,4,3,2,1:T(8,128)} reshape(f32[25,3,196,196]{0,3,2,1:T(8,128)} %copy.258) | data formatting | bytes 23049600 | tf_op jit(solution)/shard_map/reshape | solution.py:207
  1257.1 94.7 %fusion.129 = (f32[25,3,14,14,14]{0,4,3,2,1:T(8,128)}, f32[25,3,14,14,14]{0,4,3,2,1:T(8,128)}) fusion(f32[25,3,14,14,14,14]{0,5,4,3,2,1:T(8,128)} %reshape.221), kind=kLoop, calls=%fused_computation.233 | loop fusion | flops 5350800 | bytes 13171200 | tf_op jit(solution)/shard_map/reduce_sum | solution.py:208
  1419.7 24.2 %convert_element_type.249 = bf16[4,1225,576]{1,0,2:T(4,128)(2,1)} reshape(bf16[25,196,3,3,64]{1,0,4,3,2:T(8,128)(2,1)} %copy.266) | data formatting | bytes 11289600 | tf_op jit(solution)/shard_map/convert_element_type | solution.py:218
  1490.9 31.0 %all-to-all-done.10 = bf16[4,1225,576]{1,2,0:T(8,128)(2,1)} async-done(((bf16[4,1225,576]{1,2,0:T(8,128)(2,1)}), bf16[4,1225,576]{1,2,0:T(8,128)(2,1)}, u32[]{:S(2)}, u32[]{:S(2)}) %all-to-all-start.10) | async-done | bytes 5644832 | tf_op jit(solution)/shard_map/all_to_all | solution.py:107
  1612.5 106.7 %all-reduce.6.cloned.1.call-done = (f32[8,768,16]{1,2,0:T(8,128)}, f32[8,16,2304]{2,1,0:T(8,128)}, f32[8,768,16]{1,2,0:T(8,128)}, f32[8,16,768]{2,1,0:T(8,128)},...) async-done(((f32[8,768,16]{1,2,0:T(8,128)}, f32[8,16,2304]{2,1,0:T(8,128)}, f32[8,768,16]{1,2,0:T(8,128)}, ...) | async-done | bytes 6291472 | tf_op jit(solution)/shard_map/psum | solution.py:339
  (393 shorter events, 730.1 us)
Async XLA Ops:
  7.2 269.0 %copy-start = (bf16[27,64]{1,0:T(8,128)(2,1)S(1)}, bf16[27,64]{1,0:T(8,128)(2,1)}, u32[]{:S(2)}) copy-start(bf16[27,64]{1,0:T(8,128)(2,1)} %param.28) | copy-start | bytes 10372
  7.2 140.1 %all-gather.7.cloned.1.call-start = ((), (), s32[]{:S(2)}) async-start(), calls=%async_computation.12 | async-start | bytes 4423680 | tf_op jit(solution)/shard_map/all_gather | solution.py:263
  20.1 114.9 %collective-permute-start = (bf16[8,16,576]{2,1,0:T(8,128)(2,1)}, bf16[8,16,576]{2,1,0:T(8,128)(2,1)}, u32[]{:S(2)}, u32[]{:S(2)}) collective-permute-start(bf16[8,16,576]{2,1,0:T(8,128)(2,1)} %param.31), channel_id=1, source_target_pairs={{0,1},{1,2},{2,3},{3,0},{4,5},{5,6},{6,7},{7,4},{8,9},{9,10},{10,1... | collective-permute-start | bytes 442376 | tf_op jit(solution)/shard_map/ppermute | solution.py:23
  21.7 119.8 %collective-permute-start.2 = (bf16[8,16,576]{2,1,0:T(8,128)(2,1)}, bf16[8,16,576]{2,1,0:T(8,128)(2,1)}, u32[]{:S(2)}, u32[]{:S(2)}) collective-permute-start(bf16[8,16,576]{2,1,0:T(8,128)(2,1)} %param.31), channel_id=1, source_target_pairs={{0,3},{1,0},{2,1},{3,2},{4,7},{5,4},{6,5},{7,6},{8,11},{9,8},{10,9... | collective-permute-start | bytes 442376 | tf_op jit(solution)/shard_map/ppermute | solution.py:25
  45.7 101.1 %all-to-all-start = ((bf16[4,1225,192]{1,2,0:T(8,128)(2,1)}), bf16[4,1225,192]{1,2,0:T(8,128)(2,1)S(1)}, u32[]{:S(2)}, u32[]{:S(2)}) async-start(bf16[4,1225,192]{1,2,0:T(8,128)(2,1)} %copy.220), calls=%async_computation | async-start | bytes 3932160 | tf_op jit(solution)/shard_map/all_to_all | solution.py:107
  49.5 227.2 %all-gather.15.cloned.1.call-start = ((), (), s32[]{:S(2)}) async-start(), calls=%async_computation.16 | async-start | bytes 1474560 | tf_op jit(solution)/shard_map/all_gather | solution.py:282
  135.0 8.8 collective-permute-start.1
  170.6 106.0 %all-to-all-start.1 = ((bf16[1225,4,576]{0,2,1:T(8,128)(2,1)}), bf16[1225,4,576]{0,2,1:T(8,128)(2,1)}, u32[]{:S(2)}, u32[]{:S(2)}) async-start(bf16[1225,4,576]{0,2,1:T(8,128)(2,1)} %bitcast.292), calls=%async_computation.1 | async-start | bytes 11796480 | tf_op jit(solution)/shard_map/all_to_all | solution.py:111
  176.2 570.8 %all-gather.11.cloned.1.call-start = ((), (), s32[]{:S(2)}) async-start(), calls=%async_computation.14 | async-start | bytes 1474560 | tf_op jit(solution)/shard_map/all_gather | solution.py:281
  176.9 570.1 %all-gather.9.cloned.1.call-start = ((), (), s32[]{:S(2)}) async-start(), calls=%async_computation.13 | async-start | bytes 1474560 | tf_op jit(solution)/shard_map/all_gather | solution.py:264
  252.7 589.2 %all-gather.17.cloned.1.call-start = ((), (), s32[]{:S(2)}) async-start(), calls=%async_computation.17 | async-start | bytes 5898240 | tf_op jit(solution)/shard_map/all_gather | solution.py:289
  276.4 190.1 %copy-start.63 = (bf16[14,14,64,1,1]{2,1,4,3,0:T(8,128)(2,1)}, bf16[14,14,64,1,1]{2,1,4,3,0:T(8,128)(2,1)S(1)}, u32[]{:S(2)}) copy-start(bf16[14,14,64,1,1]{2,1,4,3,0:T(8,128)(2,1)S(1)} %fusion.61) | copy-start | bytes 75268
  660.8 27.9 %all-to-all-start.2 = ((bf16[4,1225,192]{1,2,0:T(8,128)(2,1)}), bf16[4,1225,192]{1,2,0:T(8,128)(2,1)S(1)}, u32[]{:S(2)}, u32[]{:S(2)}) async-start(bf16[4,1225,192]{1,2,0:T(8,128)(2,1)} %copy.237), calls=%async_computation.2 | async-start | bytes 3932160 | tf_op jit(solution)/shard_map/all_to_all | solution.py:107
  690.0 68.8 %all-to-all-start.6 = ((bf16[4,1225,192]{1,2,0:T(8,128)(2,1)}), bf16[4,1225,192]{1,2,0:T(8,128)(2,1)S(1)}, u32[]{:S(2)}, u32[]{:S(2)}) async-start(bf16[4,1225,192]{1,2,0:T(8,128)(2,1)} %copy.250), calls=%async_computation.6 | async-start | bytes 3932160 | tf_op jit(solution)/shard_map/all_to_all | solution.py:95
  693.6 187.4 %all-gather.13.cloned.1.call-start = ((), (), s32[]{:S(2)}) async-start(), calls=%async_computation.15 | async-start | bytes 5898240 | tf_op jit(solution)/shard_map/all_gather | solution.py:288
  758.8 53.6 %all-to-all-start.3 = ((bf16[1225,4,192]{0,2,1:T(8,128)(2,1)}), bf16[1225,4,192]{0,2,1:T(8,128)(2,1)}, u32[]{:S(2)}, u32[]{:S(2)}) async-start(bf16[1225,4,192]{0,2,1:T(8,128)(2,1)} %bitcast.304), calls=%async_computation.3 | async-start | bytes 3932160 | tf_op jit(solution)/shard_map/all_to_all | solution.py:115
  781.0 149.5 %copy-start.55 = (bf16[1,3072,16]{1,2,0:T(8,128)(2,1)}, bf16[1,3072,16]{1,2,0:T(8,128)(2,1)S(1)}, u32[]{:S(2)}) copy-start(bf16[1,3072,16]{1,2,0:T(8,128)(2,1)S(1)} %copy.289) | copy-start | bytes 294916
  837.2 29.0 %all-to-all-start.4 = ((bf16[4,1225,192]{1,2,0:T(8,128)(2,1)}), bf16[4,1225,192]{1,2,0:T(8,128)(2,1)}, u32[]{:S(2)}, u32[]{:S(2)}) async-start(bf16[4,1225,192]{1,2,0:T(8,128)(2,1)} %copy.244), calls=%async_computation.4 | async-start | bytes 3932160 | tf_op jit(solution)/shard_map/all_to_all | solution.py:95
  1023.7 27.9 %all-to-all-start.8 = ((bf16[4,1225,192]{1,2,0:T(8,128)(2,1)}), bf16[4,1225,192]{1,2,0:T(8,128)(2,1)S(1)}, u32[]{:S(2)}, u32[]{:S(2)}) async-start(bf16[4,1225,192]{1,2,0:T(8,128)(2,1)} %copy.253), calls=%async_computation.8 | async-start | bytes 3932160 | tf_op jit(solution)/shard_map/all_to_all | solution.py:107
  1062.4 29.3 %all-to-all-start.9 = ((bf16[1225,4,192]{0,2,1:T(8,128)(2,1)}), bf16[1225,4,192]{0,2,1:T(8,128)(2,1)}, u32[]{:S(2)}, u32[]{:S(2)}) async-start(bf16[1225,4,192]{0,2,1:T(8,128)(2,1)} %bitcast.305), calls=%async_computation.9 | async-start | bytes 3932160 | tf_op jit(solution)/shard_map/all_to_all | solution.py:111
  1091.6 358.2 %all-to-all-start.5 = ((bf16[1225,4,192]{0,2,1:T(8,128)(2,1)}), bf16[1225,4,192]{0,2,1:T(8,128)(2,1)}, u32[]{:S(2)}, u32[]{:S(2)}) async-start(bf16[1225,4,192]{0,2,1:T(8,128)(2,1)} %bitcast.38), calls=%async_computation.5 | async-start | bytes 3932160 | tf_op jit(solution)/shard_map/all_to_all | solution.py:101
  1449.8 72.1 %all-to-all-start.10 = ((bf16[4,1225,576]{1,2,0:T(8,128)(2,1)}), bf16[4,1225,576]{1,2,0:T(8,128)(2,1)}, u32[]{:S(2)}, u32[]{:S(2)}) async-start(bf16[4,1225,576]{1,2,0:T(8,128)(2,1)} %copy.267), calls=%async_computation.10 | async-start | bytes 11796480 | tf_op jit(solution)/shard_map/all_to_all | solution.py:107
  1540.4 33.6 %all-to-all-start.11 = ((bf16[1225,4,192]{0,2,1:T(8,128)(2,1)}), bf16[1225,4,192]{0,2,1:T(8,128)(2,1)}, u32[]{:S(2)}, u32[]{:S(2)}) async-start(bf16[1225,4,192]{0,2,1:T(8,128)(2,1)} %bitcast.303), calls=%async_computation.11 | async-start | bytes 3932160 | tf_op jit(solution)/shard_map/all_to_all | solution.py:115
  1544.9 174.2 %all-reduce.6.cloned.1.call-start = ((), (), s32[]{:S(2)}) async-start(), calls=%async_computation.18 | async-start | bytes 12582912 | tf_op jit(solution)/shard_map/psum | solution.py:339
  (92 other events, 1604.0 us)
Sparse Core Ops, SparseCore 0:
  20.2 70.9 all-gather.6
  92.7 15.9 all-gather.14
  178.6 23.1 all-gather.10
  252.8 28.3 all-gather.8
  282.7 88.5 all-gather.16
  747.1 100.4 all-gather.12
  1556.5 162.6 all-reduce.5
